TPU v7x, 32 devices: a whole 2x2x4 slice. The times are simulated.
32 devices in a mesh: pb: 4 (over y, core), ma: 8 (over z, x).
Axes of the slice: x: 2, y: 2, z: 4, core: 2. Of those that a mesh axis runs over, the one named last changes fastest.
Arguments:
- queries: bfloat16 [1, 1024, 2048], P(None, ('pb', 'ma')), may hold values from -6 to 6
- map_descriptors: bfloat16 [8192, 2048], P('ma', 'pb'), may hold values from -0.125 to 0.125
- slopes: int32 [8], replicated, may hold values from 0 to 15, as said below
Outputs:
- best: float32 [1, 1024, 8192], P(None, 'pb', 'ma')
Inputs may be any that keep to these rules, and one draw needn't show every extreme that they name: `slopes`: 8 distinct velocities; the largest is exactly 15.
All inputs are finite; a program needn't handle non-finite values.
Results may differ from a plain program's by a relative error of at most 0.0003.
Values may be sent and summed in bfloat16 or wider, within the bound.
A program may use at most 64 MiB of HBM per device.

v0:
```python
import math

import jax
import jax.numpy as jnp
from jax import lax
from jax.sharding import PartitionSpec as P

SEQ = 20
RAD = 10
SPAN = 285


def padded(value, sides, width):
    for axis, dim in sides:
        peers, length = (lax.axis_size(axis), value.shape[dim])
        up = [(i, (i + 1) % peers) for i in range(peers - 1)]
        down = [(j, i) for i, j in up]
        last = lax.slice_in_dim(value, length - width, length, axis=dim)
        leading = lax.slice_in_dim(value, 0, width, axis=dim)
        before = lax.ppermute(last, axis, up)
        after = lax.ppermute(leading, axis, down)
        value = jnp.concatenate([before, value, after], axis=dim)
    return value


def passed_along(value, axis, by):
    peers = lax.axis_size(axis)
    pairs = [(i, i + by) for i in range(peers) if 0 <= i + by < peers]
    return lax.ppermute(value, axis, pairs)


def score_tile(queries, map_descriptors):
    query_full = lax.all_gather(queries, "ma", axis=1, tiled=True)
    return jnp.einsum(
        "sqd,md->sqm",
        query_full,
        lax.all_gather(map_descriptors, "pb", axis=1, tiled=True),
        preferred_element_type=jnp.float32,
    )


def contrast(extended, columns):
    shape_out = (extended.shape[0], extended.shape[1], columns)
    running = jnp.zeros(shape_out, jnp.float32)
    squares = jnp.zeros(shape_out, jnp.float32)
    for offset in range(2 * RAD + 1):
        window = extended[:, :, offset : offset + columns]
        running = running + window
        squares = squares + window * window
    average = running / (2 * RAD + 1)
    spread = squares / (2 * RAD + 1) - average * average
    centre = extended[:, :, RAD : RAD + columns]
    return (centre - average) / jnp.sqrt(spread + 1.0)


def sequence_best(normal_ext, slopes, q_count, m_count):
    sessions = normal_ext.shape[0]
    best_val = None
    for slope_index in range(slopes.shape[0]):
        velocity = slopes[slope_index]
        summed = jnp.zeros((sessions, q_count, m_count), jnp.float32)
        for lag_step in range(SEQ):
            row_at = jnp.asarray(SEQ - 1 - lag_step, jnp.int32)
            col_at = SPAN - lag_step * velocity
            zero_at = jnp.asarray(0, jnp.int32)
            summed = summed + lax.dynamic_slice(
                normal_ext, (zero_at, row_at, col_at), (sessions, q_count, m_count)
            )
        best_val = summed if best_val is None else jnp.maximum(best_val, summed)
    return best_val / math.sqrt(SEQ)


def local(queries, map_descriptors, slopes):
    m_count = map_descriptors.shape[0]
    lead_rows = SEQ - 1
    scores = score_tile(queries, map_descriptors)
    q_count = scores.shape[1]
    widened = padded(scores, (("ma", 2),), RAD)
    normal = contrast(widened, m_count)
    before = passed_along(normal[:, :, m_count - SPAN :], "ma", 1)
    normal_ext = jnp.concatenate([before, normal], axis=2)
    above = passed_along(normal_ext[:, q_count - lead_rows :], "pb", 1)
    normal_ext = jnp.concatenate([above, normal_ext], axis=1)
    return sequence_best(normal_ext, slopes, q_count, m_count)


def solution(mesh):
    return jax.shard_map(
        local,
        mesh=mesh,
        in_specs=(P(None, ("pb", "ma"), None), P("ma", "pb"), P()),
        out_specs=P(None, "pb", "ma"),
        check_vma=False,
    )
```

profile of v0, /device:TPU:13, one launch (start us, length us, event | category | flops | bytes accessed | tf_op | source)
XLA Modules:
  0.0 366.3 jit_solution(10224925232081690869)
XLA Ops:
  6.5 0.0 all-gather.3.cloned.1.call-start
  6.5 0.7 all-gather.3.cloned.1.call-update
  7.3 0.0 all-gather.5.cloned.1.call-start
  7.3 0.7 all-gather.5.cloned.1.call-update
  8.0 41.0 %all-gather.3.cloned.1.call-done = bf16[1,256,2048]{2,1,0:T(8,128)(2,1)} async-done(((bf16[1,32,2048]{2,1,0:T(8,128)(2,1)}), bf16[1,256,2048]{2,1,0:T(8,128)(2,1)}) %all-gather.3.cloned.1.call-update) | async-done | bytes 1048592 | tf_op jit(solution)/shard_map/all_gather | solution.py:33
  49.0 36.1 %all-gather.5.cloned.1.call-done = bf16[1024,2048]{1,0:T(8,128)(2,1)} async-done(((bf16[1024,512]{1,0:T(8,128)(2,1)}), bf16[1024,2048]{1,0:T(8,128)(2,1)}) %all-gather.5.cloned.1.call-update) | async-done | bytes 4194320 | tf_op jit(solution)/shard_map/all_gather | solution.py:37
  85.1 3.8 %fusion.345 = f32[256,1024]{1,0:T(8,128)S(1)} fusion(bf16[1024,2048]{1,0:T(8,128)(2,1)} %all-gather.5.cloned.1.call-done, bf16[1,256,2048]{2,1,0:T(8,128)(2,1)} %all-gather.3.cloned.1.call-done), kind=kOutput, calls=%fused_computation.539 | convolution fusion | flops 1073741824 | bytes 6291456 | tf_op jit(solution)/shard_map/sqd,md->sqm/dot_general | solution.py:34
  88.9 0.1 fusion.348
  89.0 3.1 collective-permute-start
  92.1 0.0 copy-start
  92.1 3.1 collective-permute-start.1
  95.2 1.4 collective-permute-done
  96.6 3.1 collective-permute-done.1
  99.7 7.6 %fusion.344 = f32[1,256,1024]{2,1,0:T(8,128)S(1)} fusion(f32[256,1024]{1,0:T(8,128)S(1)} %fusion.345, f32[1,256,1024]{2,1,0:T(8,128)S(1)} %bitcast.342, f32[1,256,10]{2,1,0:T(8,128)S(1)} %collective-permute-done.1, f32[1,256,10]{2,1,0:T(8,128)S(1)} %collective-permute-done), kind=kLoop, calls=%fused_computation.538 | loop fusion | flops 23068672 | bytes 3166208 | tf_op jit(solution)/shard_map/div | solution.py:53
  107.3 0.2 slice.186
  107.5 2.8 collective-permute-start.2
  110.3 0.0 copy-done
  110.3 0.7 fusion.349
  213.7 0.0 collective-permute-done.2
  213.8 0.1 fusion.347
  213.9 1.3 collective-permute-start.3
  215.2 0.4 pad_maximum_fusion
  215.5 2.8 collective-permute-done.3
  218.3 141.2 %fusion.21 = f32[1,256,1024]{2,1,0:T(8,128)} fusion(s32[]{:T(128)S(6)} %select_n.607, f32[1,19,1309]{2,1,0:T(8,128)S(1)} %collective-permute-done.3, f32[1,256,1024]{2,1,0:T(8,128)S(1)} %fusion.344, s32[]{:T(128)S(6)} %select_n.532, s32[]{:T(128)S(6)} %select_n.533, s32[]{:T(128)S(6)} %select_n.534, s32[]{:T(128)S(6)} %select_n.535, s32[]{:T(128)S(6)} %select_n.536, ...), kind=kLoop, calls=%fused_computation.212 | loop fusion | flops 81788928 | bytes 3537660 | tf_op jit(solution)/shard_map/div | solution.py:70
Async XLA Ops:
  6.5 42.5 %all-gather.3.cloned.1.call-start = ((), (), s32[]{:S(2)}) async-start(), calls=%async_computation | async-start | bytes 1179648 | tf_op jit(solution)/shard_map/all_gather | solution.py:33
  7.3 77.9 %all-gather.5.cloned.1.call-start = ((), (), s32[]{:S(2)}) async-start(), calls=%async_computation.1 | async-start | bytes 5242880 | tf_op jit(solution)/shard_map/all_gather | solution.py:37
  89.0 7.6 %collective-permute-start = (f32[1,256,10]{2,1,0:T(8,128)S(1)}, f32[1,256,10]{2,1,0:T(8,128)S(1)}, u32[]{:S(2)}, u32[]{:S(2)}) collective-permute-start(f32[1,256,10]{2,1,0:T(8,128)S(1)} %get-tuple-element.5), channel_id=1, source_target_pairs={{0,1},{1,2},{2,3},{3,4},{4,5},{5,6},{6,7},{8,9},{9,10},{10,11},{11... | collective-permute-start | bytes 30728 | tf_op jit(solution)/shard_map/ppermute | solution.py:20
  92.1 18.2 %copy-start = (s32[8]{0:T(128)S(1)}, s32[8]{0:T(128)}, u32[]{:S(2)}) copy-start(s32[8]{0:T(128)} %param.5) | copy-start | bytes 100
  92.1 7.6 %collective-permute-start.1 = (f32[1,256,10]{2,1,0:T(8,128)S(1)}, f32[1,256,10]{2,1,0:T(8,128)S(1)}, u32[]{:S(2)}, u32[]{:S(2)}) collective-permute-start(f32[1,256,10]{2,1,0:T(8,128)S(1)} %get-tuple-element.6), channel_id=1, source_target_pairs={{1,0},{2,1},{3,2},{4,3},{5,4},{6,5},{7,6},{9,8},{10,9},{11,10},{12... | collective-permute-start | bytes 30728 | tf_op jit(solution)/shard_map/ppermute | solution.py:21
  107.5 106.3 %collective-permute-start.2 = (f32[1,256,285]{2,1,0:T(8,128)S(1)}, f32[1,256,285]{2,1,0:T(8,128)S(1)}, u32[]{:S(2)}, u32[]{:S(2)}) collective-permute-start(f32[1,256,285]{2,1,0:T(8,128)S(1)} %slice.186), channel_id=1, source_target_pairs={{0,1},{1,2},{2,3},{3,4},{4,5},{5,6},{6,7},{8,9},{9,10},{10,11},{11... | collective-permute-start | bytes 875528 | tf_op jit(solution)/shard_map/ppermute | solution.py:29
  213.9 4.4 %collective-permute-start.3 = (f32[1,19,1309]{2,1,0:T(8,128)S(1)}, f32[1,19,1309]{2,1,0:T(8,128)S(1)}, u32[]{:S(2)}, u32[]{:S(2)}) collective-permute-start(f32[1,19,1309]{2,1,0:T(8,128)S(1)} %fusion.347), channel_id=1, source_target_pairs={{0,8},{8,16},{16,24},{1,9},{9,17},{17,25},{2,10},{10,18},{18,26},{... | collective-permute-start | bytes 298460 | tf_op jit(solution)/shard_map/ppermute | solution.py:29
Sparse Core Ops, SparseCore 0:
  9.5 39.5 all-gather.2
  50.6 34.4 all-gather.4
where the time goes:
time: 371 us; the launch traced here: 366 us
  other arithmetic  149 us (40%)
  between operations  116 us (31%)
  waiting for transfers between devices  85.8 us (23%)
  starting transfers between devices  10.3 us (3%)
  matrix products  3.79 us (1%)
    div x1, other arithmetic, sequence_best(): return best_val / math.sqrt(SEQ)  141 us
    all_gather x1, waiting for transfers between devices, score_tile(): query_full = lax.all_gather(queries, 'ma', axis=1, tiled=True)  41 us
    all_gather x1, waiting for transfers between devices, score_tile(): lax.all_gather(map_descriptors, 'pb', axis=1, tiled=True)  36.1 us
    div x1, other arithmetic, contrast(): return (centre - average) / jnp.sqrt(spread + 1.0)  7.57 us
  transfers between devices with their start and end apart: 6, of which 5 were waited for; matrix products, arithmetic and copies ran while one was open for 0% of the time, Pallas kernels for 0%

commit v1 on v0

v1 whole, which is shorter than its diff:
```python
import math

import jax
import jax.numpy as jnp
from jax import lax
from jax.experimental import pallas as pl
from jax.experimental.pallas import tpu as pltpu
from jax.sharding import PartitionSpec as P

MESH = pl.DeviceIdType.MESH
SEQ = 20
RAD = 10
LEAD = 32
LEFT = 384
RIGHT = 128
LANES = 128
CORES = 2


def remote(src, dst, send, recv, where):
    return pltpu.make_async_remote_copy(
        src_ref=src,
        dst_ref=dst,
        send_sem=send,
        recv_sem=recv,
        device_id=where,
        device_id_type=MESH,
    )


def score_kernel(
    npb,
    nma,
    chunks,
    q_ref,
    m_ref,
    out_ref,
    q_all,
    q_lead,
    m_all,
    scores,
    left,
    right,
    local_sem,
    q_send,
    q_recv,
    lead_sem,
    m_send,
    m_recv,
    halo_send,
    halo_recv,
):
    pb, ma = lax.axis_index("pb"), lax.axis_index("ma")
    pair, across = npb // CORES, nma // 2
    row, core = pb // CORES, pb % CORES
    z, x = ma // 2, ma % 2
    mate = row * CORES + 1 - core
    twin = z * 2 + 1 - x
    rows_other = [((row + i) % pair) * CORES + core for i in range(1, pair)]
    rows_from = [((row + pair - i) % pair) * CORES + core for i in range(1, pair)]
    z_other = [((z + i) % across) * 2 + x for i in range(1, across)]
    z_from = [((z + across - i) % across) * 2 + x for i in range(1, across)]
    has_up, has_down = pb > 0, pb < npb - 1
    has_left, has_right = ma > 0, ma < nma - 1

    load_q = pltpu.make_async_copy(q_ref.at[0], q_all.at[ma], local_sem.at[0])
    load_q.start()
    load_m = pltpu.make_async_copy(m_ref, m_all.at[pb], local_sem.at[1])
    load_m.start()

    barrier = pltpu.get_barrier_semaphore()

    def greet(where):
        pl.semaphore_signal(barrier, inc=1, device_id=where, device_id_type=MESH)

    greet({"pb": mate})
    greet({"ma": twin})
    for other in rows_other:
        greet({"pb": other})
    for other in z_other:
        greet({"ma": other})
    for test, where in (
        (has_up, {"pb": pb - 1}),
        (has_down, {"pb": pb + 1}),
        (has_left, {"ma": ma - 1}),
        (has_right, {"ma": ma + 1}),
    ):

        @pl.when(test)
        def _():
            greet(where)

    edges = sum(
        jnp.where(test, 1, 0) for test in (has_up, has_down, has_left, has_right)
    )
    pl.semaphore_wait(barrier, pair + across + edges)

    load_q.wait()
    q_to_z = [
        remote(q_all.at[ma], q_all.at[ma], q_send.at[i], q_recv.at[i], {"ma": other})
        for i, other in enumerate(z_other)
    ]
    for copy in q_to_z:
        copy.start()
    first = across - 1
    q_to_x = [
        remote(
            q_all.at[ma], q_all.at[ma], q_send.at[first], q_recv.at[first], {"ma": twin}
        )
    ]
    q_to_x[0].start()

    load_m.wait()
    m_count = m_ref.shape[0]
    step = m_count // chunks
    order = list(range(chunks - 1, chunks // 2 - 1, -1)) + list(range(chunks // 2))

    def piece(slot, chunk):
        return m_all.at[slot, pl.ds(chunk * step, step)]

    m_to_row, m_to_mate = {}, {}
    for chunk in order:
        for i, other in enumerate(rows_other):
            at = i * chunks + chunk
            m_to_row[i, chunk] = remote(
                piece(pb, chunk), piece(pb, chunk), m_send.at[at], m_recv.at[at], {"pb": other}
            )
            m_to_row[i, chunk].start()
    for chunk in order:
        at = (pair - 1) * chunks + chunk
        m_to_mate[-1, chunk] = remote(
            piece(pb, chunk), piece(pb, chunk), m_send.at[at], m_recv.at[at], {"pb": mate}
        )
        m_to_mate[-1, chunk].start()

    for i, source in enumerate(z_from):
        q_to_z[i].wait_recv()
        at = across + i
        copy = remote(
            q_all.at[source], q_all.at[source], q_send.at[at], q_recv.at[at], {"ma": twin}
        )
        copy.start()
        q_to_x.append(copy)
    for copy in q_to_x:
        copy.wait_recv()

    held = q_lead.shape[0]
    lead = remote(
        q_all.at[pl.ds(nma - held, held)], q_lead, lead_sem.at[0], lead_sem.at[1], {"pb": pb + 1}
    )

    @pl.when(has_down)
    def _():
        lead.start()

    @pl.when(pb == 0)
    def _():
        q_lead[...] = jnp.zeros_like(q_lead)

    @pl.when(ma == 0)
    def _():
        left[...] = jnp.zeros_like(left)

    @pl.when(ma == nma - 1)
    def _():
        right[...] = jnp.zeros_like(right)

    def flat(ref):
        count, each, width = ref.shape
        if each % 16 == 0:
            return ref[...].reshape(count * each, width)
        return ref[...].astype(jnp.float32).reshape(count * each, width).astype(ref.dtype)

    to_right = remote(
        scores.at[:, pl.ds(m_count - LEFT, LEFT)],
        left,
        halo_send.at[0],
        halo_recv.at[0],
        {"ma": ma + 1},
    )
    to_left = remote(
        scores.at[:, pl.ds(0, RIGHT)],
        right,
        halo_send.at[1],
        halo_recv.at[1],
        {"ma": ma - 1},
    )
    done = set()
    for number, chunk in enumerate(order):
        for i, source in enumerate(rows_from):
            m_to_row[i, chunk].wait_recv()
            at = (pair + i) * chunks + chunk
            m_to_mate[i, chunk] = remote(
                piece(source, chunk), piece(source, chunk), m_send.at[at], m_recv.at[at], {"pb": mate}
            )
            m_to_mate[i, chunk].start()
        for i in range(-1, pair - 1):
            m_to_mate[i, chunk].wait_recv()
        if number == 0:

            @pl.when(has_up)
            def _():
                lead.wait_recv()

        k = m_ref.shape[1]
        for queries, at in ((q_lead, 0), (q_all, LEAD)):
            total = None
            block = flat(queries)
            for slot in range(npb):
                part = lax.dot_general(
                    block[:, slot * k : (slot + 1) * k],
                    m_all[slot, pl.ds(chunk * step, step), :],
                    (((1,), (1,)), ((), ())),
                    preferred_element_type=jnp.float32,
                )
                total = part if total is None else total + part
            scores[pl.ds(at, block.shape[0]), pl.ds(chunk * step, step)] = total
        before = set(done)
        done.update(range(chunk * step, (chunk + 1) * step, LANES))
        right_part = set(range(m_count - LEFT, m_count, LANES))
        left_part = set(range(0, RIGHT, LANES))
        if right_part <= done and not right_part <= before:

            @pl.when(has_right)
            def _():
                to_right.start()

        if left_part <= done and not left_part <= before:

            @pl.when(has_left)
            def _():
                to_left.start()

    out_ref[:, pl.ds(LEFT, m_count)] = scores[...]

    @pl.when(has_left)
    def _():
        to_right.wait_recv()

    out_ref[:, pl.ds(0, LEFT)] = left[...]

    @pl.when(has_right)
    def _():
        to_left.wait_recv()

    out_ref[:, pl.ds(LEFT + m_count, RIGHT)] = right[...]

    for copy in q_to_z + q_to_x + list(m_to_row.values()) + list(m_to_mate.values()):
        copy.wait_send()

    @pl.when(has_down)
    def _():
        lead.wait_send()

    @pl.when(has_right)
    def _():
        to_right.wait_send()

    @pl.when(has_left)
    def _():
        to_left.wait_send()


def score_tile(queries, map_descriptors, npb, nma):
    each, width = queries.shape[1:]
    m_count, k = map_descriptors.shape
    q_count = each * nma
    chunks = 4
    held = LEAD // each
    pair, across = npb // CORES, nma // 2
    dma = pltpu.SemaphoreType.DMA
    return pl.pallas_call(
        lambda *refs: score_kernel(npb, nma, chunks, *refs),
        out_shape=jax.ShapeDtypeStruct(
            (LEAD + q_count, LEFT + m_count + RIGHT), jnp.float32
        ),
        in_specs=[pl.BlockSpec(memory_space=pl.ANY)] * 2,
        out_specs=pl.BlockSpec(memory_space=pltpu.VMEM),
        scratch_shapes=[
            pltpu.VMEM((nma, each, width), jnp.bfloat16),
            pltpu.VMEM((held, each, width), jnp.bfloat16),
            pltpu.VMEM((npb, m_count, k), jnp.bfloat16),
            pltpu.VMEM((LEAD + q_count, m_count), jnp.float32),
            pltpu.VMEM((LEAD + q_count, LEFT), jnp.float32),
            pltpu.VMEM((LEAD + q_count, RIGHT), jnp.float32),
            dma((2,)),
            dma((2 * across,)),
            dma((2 * across,)),
            dma((2,)),
            dma((2 * pair * chunks,)),
            dma((2 * pair * chunks,)),
            dma((2,)),
            dma((2,)),
        ],
        compiler_params=pltpu.CompilerParams(
            collective_id=0, has_side_effects=True, vmem_limit_bytes=48 << 20
        ),
        name="scores",
    )(queries, map_descriptors)


def best_kernel(slopes_ref, ext_ref, out_ref, c_ref, a2_ref, a4_ref, a8_ref):
    pb, ma = lax.axis_index("pb"), lax.axis_index("ma")
    rows, width = ext_ref.shape
    q_count, m_count = rows - LEAD, width - LEFT - RIGHT
    halo = LEFT // LANES
    tiles = halo + m_count // LANES
    size = 2 * RAD + 1

    def window(value):
        two = value + pltpu.roll(value, 1, 1)
        four = two + pltpu.roll(two, 2, 1)
        eight = four + pltpu.roll(four, 4, 1)
        sixteen = eight + pltpu.roll(eight, 8, 1)
        total = sixteen + pltpu.roll(four, 16, 1) + pltpu.roll(value, 20, 1)
        return pltpu.roll(total, width - RAD, 1) * (1.0 / size)

    group = 16
    first_row = jnp.where(pb == 0, LEAD, 0)
    first_col = jnp.where(ma == 0, LEFT, 0)

    @pl.loop(0, rows // group)
    def _(number):
        at = pl.multiple_of(number * group, group)
        value = ext_ref[pl.ds(at, group), :]
        average = window(value)
        spread = window(value * value) - average * average
        normal = (value - average) * (lax.rsqrt(spread + 1.0) * (1.0 / math.sqrt(SEQ)))
        row = lax.broadcasted_iota(jnp.int32, (group, width), 0) + at
        col = lax.broadcasted_iota(jnp.int32, (group, width), 1)
        normal = jnp.where((row >= first_row) & (col >= first_col), normal, 0.0)
        for tile in range(tiles):
            c_ref[tile, pl.ds(at, group), :] = normal[:, tile * LANES : (tile + 1) * LANES]

    out_ref[0] = jnp.full((q_count, m_count), -jnp.inf, jnp.float32)

    def moved(ref, tile, at, count, shift, lane, before):
        here = pltpu.roll(ref[tile, pl.ds(at, count), :], shift, 1)
        return here, jnp.where(lane < shift, here if before is None else before, here)

    def add(dst, src, lag, shift, start, count, low):
        lane = lax.broadcasted_iota(jnp.int32, (count, LANES), 1)

        @pl.loop(0, (rows - start) // count)
        def _(number):
            at = pl.multiple_of(start + number * count, 8)
            before = None
            if low > 0:
                before = pltpu.roll(src[low - 1, pl.ds(at - lag, count), :], shift, 1)
            for tile in range(low, tiles):
                before, other = moved(src, tile, at - lag, count, shift, lane, before)
                dst[tile, pl.ds(at, count), :] = src[tile, pl.ds(at, count), :] + other

    @pl.loop(0, slopes_ref.shape[0])
    def _(index):
        v = slopes_ref[index]
        add(a2_ref, c_ref, 1, v, 8, 40, 0)
        add(a4_ref, a2_ref, 2, 2 * v, 16, 16, halo - 2)
        add(a8_ref, a4_ref, 4, 4 * v, 24, 24, halo - 1)
        far = 16 * v
        back, rest = far // LANES, far % LANES
        count = 32
        lane = lax.broadcasted_iota(jnp.int32, (count, LANES), 1)

        @pl.loop(0, q_count // count)
        def _(number):
            at = pl.multiple_of(LEAD + number * count, 8)
            low = halo - 1
            before8 = pltpu.roll(a8_ref[low, pl.ds(at - 8, count), :], 8 * v, 1)
            before4 = pltpu.roll(a4_ref[low - back, pl.ds(at - 16, count), :], rest, 1)
            for tile in range(halo, tiles):
                before8, eight = moved(a8_ref, tile, at - 8, count, 8 * v, lane, before8)
                before4, four = moved(a4_ref, tile - back, at - 16, count, rest, lane, before4)
                total = a8_ref[tile, pl.ds(at, count), :] + eight + four
                to = pl.multiple_of(number * count, 8)
                cols = pl.ds((tile - halo) * LANES, LANES)
                out_ref[0, pl.ds(to, count), cols] = jnp.maximum(
                    out_ref[0, pl.ds(to, count), cols], total
                )


def sequence_best(extended, slopes):
    rows, width = extended.shape
    m_count = width - LEFT - RIGHT
    tiles = (LEFT + m_count) // LANES
    return pl.pallas_call(
        best_kernel,
        out_shape=jax.ShapeDtypeStruct((1, rows - LEAD, m_count), jnp.float32),
        in_specs=[
            pl.BlockSpec(memory_space=pltpu.SMEM),
            pl.BlockSpec(memory_space=pltpu.VMEM),
        ],
        out_specs=pl.BlockSpec(memory_space=pltpu.VMEM),
        scratch_shapes=[pltpu.VMEM((tiles, rows, LANES), jnp.float32)] * 4,
        compiler_params=pltpu.CompilerParams(vmem_limit_bytes=32 << 20),
        name="best",
    )(slopes, extended)


def solution(mesh):
    npb, nma = mesh.shape["pb"], mesh.shape["ma"]

    def local(queries, map_descriptors, slopes):
        return sequence_best(score_tile(queries, map_descriptors, npb, nma), slopes)

    return jax.shard_map(
        local,
        mesh=mesh,
        in_specs=(P(None, ("pb", "ma"), None), P("ma", "pb"), P()),
        out_specs=P(None, "pb", "ma"),
        check_vma=False,
    )
```

time: 371 us -> 103 us (0.28); the launches traced: 366 us -> 102 us
  other arithmetic: 149 us -> 0 us
  between operations: 116 us -> 0.02 us
  Pallas kernels: 0 us -> 100 us
  waiting for transfers between devices: 85.8 us -> 0 us
  starting transfers between devices: 10.3 us -> 0 us
  matrix products: 3.79 us -> 0 us
    div x2 -> x0, other arithmetic: 149 us -> none  [the longest x1 141 us: sequence_best(): return best_val / math.sqrt(SEQ)]
    pallas_call x0 -> x2, Pallas kernels: none -> 100 us  [the longest x1 53.9 us: sequence_best(): pl.pallas_call(best_kernel, out_shape=jax.ShapeDtypeStruct((1, rows - LEA...]
    all_gather x2 -> x0, waiting for transfers between devices: 77.1 us -> none  [the longest x1 41 us: score_tile(): query_full = lax.all_gather(queries, 'ma', axis=1, tiled=True)]
    ppermute x4 -> x0, starting transfers between devices: 10.3 us -> none  [the longest x2 4.11 us: passed_along(): return lax.ppermute(value, axis, pairs)]
    ppermute x4 -> x0, waiting for transfers between devices: 7.24 us -> none  [the longest x1 3.13 us: padded(): after = lax.ppermute(leading, axis, down)]
    dot_general x1 -> x0, matrix products: 3.79 us -> none  [score_tile(): jnp.einsum('sqd,md->sqm', query_full, lax.all_gather(map_descriptors, 'pb...]
  transfers between devices with their start and end apart: 6 -> 0, of which waited for: 5 -> 0; matrix products, arithmetic and copies ran while one was open for 0% -> 0% of each run, Pallas kernels for 0% -> 0%
where the time goes in v1:
time: 103 us; the launch traced here: 102 us
  Pallas kernels  100 us (97%)
  local copies, waits for them, and re-layouts  2.13 us (2%)
    pallas_call x1, Pallas kernels, sequence_best(): pl.pallas_call(best_kernel, out_shape=jax.ShapeDtypeStruct((1, rows - LEA...  53.9 us
    pallas_call x1, Pallas kernels, score_tile(): pl.pallas_call(lambda *refs: score_kernel(npb, nma, chunks, *refs), out_s...  46.4 us
    unnamed x6, local copies, waits for them, and re-layouts  2.13 us

profile of v1, /device:TPU:13, one launch (start us, length us, event | category | flops | bytes accessed | tf_op | source)
XLA Modules:
  0.0 102.4 jit_solution(1286643299715269255)
XLA Ops:
  0.0 0.0 copy-start
  0.0 1.2 %copy-done = bf16[1024,512]{1,0:T(8,128)(2,1)S(1)} copy-done((bf16[1024,512]{1,0:T(8,128)(2,1)S(1)}, bf16[1024,512]{1,0:T(8,128)(2,1)}, u32[]{:S(2)}) %copy-start) | copy-done | bytes 1048600
  1.2 0.0 copy-start.1
  1.2 0.9 copy-done.1
  2.1 0.0 copy-start.2
  2.1 46.4 %scores.1.ext_ref = f32[288,1536]{1,0:T(8,128)S(1)} custom-call(bf16[1,32,2048]{2,1,0:T(8,128)(2,1)S(1)} %copy-done.1, bf16[1024,512]{1,0:T(8,128)(2,1)S(1)} %copy-done), custom_call_target="tpu_custom_call" | custom-call | tf_op jit(solution)/shard_map/scores/pallas_call | solution.py:272
  48.5 0.0 copy-done.2
  48.5 53.9 %best.1 = f32[1,256,1024]{2,1,0:T(8,128)} custom-call(s32[8]{0:T(128)S(1)} %copy-done.2, f32[288,1536]{1,0:T(8,128)S(1)} %scores.1.ext_ref), custom_call_target="tpu_custom_call" | custom-call | tf_op jit(solution)/shard_map/best/pallas_call | solution.py:386
Async XLA Ops:
  0.0 1.2 %copy-start = (bf16[1024,512]{1,0:T(8,128)(2,1)S(1)}, bf16[1024,512]{1,0:T(8,128)(2,1)}, u32[]{:S(2)}) copy-start(bf16[1024,512]{1,0:T(8,128)(2,1)} %refs_1_.1) | copy-start | bytes 3145732
  1.2 0.9 copy-start.1
  2.1 46.4 %copy-start.2 = (s32[8]{0:T(128)S(1)}, s32[8]{0:T(128)}, u32[]{:S(2)}) copy-start(s32[8]{0:T(128)} %slopes_ref.1) | copy-start | bytes 100

commit v2 on v1

--- a/solution.py
+++ b/solution.py
@@ -338,12 +338,10 @@
         here = pltpu.roll(ref[tile, pl.ds(at, count), :], shift, 1)
         return here, jnp.where(lane < shift, here if before is None else before, here)
 
-    def add(dst, src, lag, shift, start, count, low):
+    def add(dst, src, lag, shift, base, start, count, low):
         lane = lax.broadcasted_iota(jnp.int32, (count, LANES), 1)
-
-        @pl.loop(0, (rows - start) // count)
-        def _(number):
-            at = pl.multiple_of(start + number * count, 8)
+        for first in range(start, rows, count):
+            at = base + first
             before = None
             if low > 0:
                 before = pltpu.roll(src[low - 1, pl.ds(at - lag, count), :], shift, 1)
@@ -354,17 +352,16 @@
     @pl.loop(0, slopes_ref.shape[0])
     def _(index):
         v = slopes_ref[index]
-        add(a2_ref, c_ref, 1, v, 8, 40, 0)
-        add(a4_ref, a2_ref, 2, 2 * v, 16, 16, halo - 2)
-        add(a8_ref, a4_ref, 4, 4 * v, 24, 24, halo - 1)
+        base = pl.multiple_of((v // 16) * 8, 8)
+        add(a2_ref, c_ref, 1, v, base, 8, 40, 0)
+        add(a4_ref, a2_ref, 2, 2 * v, base, 16, 16, halo - 2)
+        add(a8_ref, a4_ref, 4, 4 * v, base, 24, 24, halo - 1)
         far = 16 * v
         back, rest = far // LANES, far % LANES
-        count = 32
+        count = 16
         lane = lax.broadcasted_iota(jnp.int32, (count, LANES), 1)
-
-        @pl.loop(0, q_count // count)
-        def _(number):
-            at = pl.multiple_of(LEAD + number * count, 8)
+        for first in range(0, q_count, count):
+            at = base + (LEAD + first)
             low = halo - 1
             before8 = pltpu.roll(a8_ref[low, pl.ds(at - 8, count), :], 8 * v, 1)
             before4 = pltpu.roll(a4_ref[low - back, pl.ds(at - 16, count), :], rest, 1)
@@ -372,10 +369,9 @@
                 before8, eight = moved(a8_ref, tile, at - 8, count, 8 * v, lane, before8)
                 before4, four = moved(a4_ref, tile - back, at - 16, count, rest, lane, before4)
                 total = a8_ref[tile, pl.ds(at, count), :] + eight + four
-                to = pl.multiple_of(number * count, 8)
                 cols = pl.ds((tile - halo) * LANES, LANES)
-                out_ref[0, pl.ds(to, count), cols] = jnp.maximum(
-                    out_ref[0, pl.ds(to, count), cols], total
+                out_ref[0, pl.ds(first, count), cols] = jnp.maximum(
+                    out_ref[0, pl.ds(first, count), cols], total
                 )
 
 

time: 103 us -> 79.2 us (0.77)
  Pallas kernels: 100 us -> 76.9 us
    pallas_call x1, Pallas kernels: 53.9 us -> 30.6 us  [sequence_best(): pl.pallas_call(best_kernel, out_shape=jax.ShapeDtypeStruct((1, rows - LEA...]
where the time goes in v2:
time: 79.2 us; the launch traced here: 79.1 us
  Pallas kernels  76.9 us (97%)
  local copies, waits for them, and re-layouts  2.13 us (3%)
    pallas_call x1, Pallas kernels, score_tile(): pl.pallas_call(lambda *refs: score_kernel(npb, nma, chunks, *refs), out_s...  46.4 us
    pallas_call x1, Pallas kernels, sequence_best(): pl.pallas_call(best_kernel, out_shape=jax.ShapeDtypeStruct((1, rows - LEA...  30.6 us
    unnamed x6, local copies, waits for them, and re-layouts  2.13 us

profile of v2, /device:TPU:13, one launch (start us, length us, event | category | flops | bytes accessed | tf_op | source)
XLA Modules:
  0.0 79.1 jit_solution(2609683203377248402)
XLA Ops:
  0.0 0.0 copy-start
  0.0 1.2 %copy-done = bf16[1024,512]{1,0:T(8,128)(2,1)S(1)} copy-done((bf16[1024,512]{1,0:T(8,128)(2,1)S(1)}, bf16[1024,512]{1,0:T(8,128)(2,1)}, u32[]{:S(2)}) %copy-start) | copy-done | bytes 1048600
  1.2 0.0 copy-start.1
  1.2 0.9 %copy-done.1 = bf16[1,32,2048]{2,1,0:T(8,128)(2,1)S(1)} copy-done((bf16[1,32,2048]{2,1,0:T(8,128)(2,1)S(1)}, bf16[1,32,2048]{2,1,0:T(8,128)(2,1)}, u32[]{:S(2)}) %copy-start.1) | copy-done | bytes 131096
  2.1 0.0 copy-start.2
  2.1 46.4 %scores.1.ext_ref = f32[288,1536]{1,0:T(8,128)S(1)} custom-call(bf16[1,32,2048]{2,1,0:T(8,128)(2,1)S(1)} %copy-done.1, bf16[1024,512]{1,0:T(8,128)(2,1)S(1)} %copy-done), custom_call_target="tpu_custom_call" | custom-call | tf_op jit(solution)/shard_map/scores/pallas_call | solution.py:272
  48.5 0.0 copy-done.2
  48.5 30.6 %best.1 = f32[1,256,1024]{2,1,0:T(8,128)} custom-call(s32[8]{0:T(128)S(1)} %copy-done.2, f32[288,1536]{1,0:T(8,128)S(1)} %scores.1.ext_ref), custom_call_target="tpu_custom_call" | custom-call | tf_op jit(solution)/shard_map/best/pallas_call | solution.py:382
Async XLA Ops:
  0.0 1.2 %copy-start = (bf16[1024,512]{1,0:T(8,128)(2,1)S(1)}, bf16[1024,512]{1,0:T(8,128)(2,1)}, u32[]{:S(2)}) copy-start(bf16[1024,512]{1,0:T(8,128)(2,1)} %refs_1_.1) | copy-start | bytes 3145732
  1.2 0.9 %copy-start.1 = (bf16[1,32,2048]{2,1,0:T(8,128)(2,1)S(1)}, bf16[1,32,2048]{2,1,0:T(8,128)(2,1)}, u32[]{:S(2)}) copy-start(bf16[1,32,2048]{2,1,0:T(8,128)(2,1)} %refs_0_.1) | copy-start | bytes 393220
  2.1 46.4 %copy-start.2 = (s32[8]{0:T(128)S(1)}, s32[8]{0:T(128)}, u32[]{:S(2)}) copy-start(s32[8]{0:T(128)} %slopes_ref.1) | copy-start | bytes 100

commit v3 on v2

--- a/solution.py
+++ b/solution.py
@@ -307,30 +307,53 @@
     tiles = halo + m_count // LANES
     size = 2 * RAD + 1
 
-    def window(value):
-        two = value + pltpu.roll(value, 1, 1)
-        four = two + pltpu.roll(two, 2, 1)
-        eight = four + pltpu.roll(four, 4, 1)
-        sixteen = eight + pltpu.roll(eight, 8, 1)
-        total = sixteen + pltpu.roll(four, 16, 1) + pltpu.roll(value, 20, 1)
-        return pltpu.roll(total, width - RAD, 1) * (1.0 / size)
-
-    group = 16
+    block = 2 * LANES
+
+    def band_of(depth, width, lead):
+        inner = lax.broadcasted_iota(jnp.int32, (depth, width), 0)
+        outer = lax.broadcasted_iota(jnp.int32, (depth, width), 1)
+        near = jnp.abs(inner - lead - outer) <= RAD
+        return jnp.where(near, 1.0, 0.0).astype(jnp.bfloat16)
+
+    def window(value, band):
+        total = None
+        for _ in range(3):
+            part = value.astype(jnp.bfloat16)
+            value = value - part.astype(jnp.float32)
+            term = jnp.dot(part, band, preferred_element_type=jnp.float32)
+            total = term if total is None else total + term
+        return total * (1.0 / size)
+
+    group = 96
     first_row = jnp.where(pb == 0, LEAD, 0)
     first_col = jnp.where(ma == 0, LEFT, 0)
+    edge = band_of(block, LANES, 0)
+    inside = band_of(2 * block, block, LANES)
+
+    def contrast(at, tile, lead, count, band):
+        begin = tile * LANES - lead
+        value = ext_ref[pl.ds(at, group), pl.ds(begin, band.shape[0])]
+        centre = value[:, lead : lead + count * LANES]
+        average = window(value, band)
+        spread = window(value * value, band) - average * average
+        normal = (centre - average) * (
+            lax.rsqrt(spread + 1.0) * (1.0 / math.sqrt(SEQ))
+        )
+        row = lax.broadcasted_iota(jnp.int32, normal.shape, 0) + at
+        col = lax.broadcasted_iota(jnp.int32, normal.shape, 1) + tile * LANES
+        seen = (row >= first_row) & (col >= first_col)
+        normal = jnp.where(seen, normal, 0.0)
+        for half in range(count):
+            c_ref[tile + half, pl.ds(at, group), :] = normal[
+                :, half * LANES : (half + 1) * LANES
+            ]
 
     @pl.loop(0, rows // group)
     def _(number):
-        at = pl.multiple_of(number * group, group)
-        value = ext_ref[pl.ds(at, group), :]
-        average = window(value)
-        spread = window(value * value) - average * average
-        normal = (value - average) * (lax.rsqrt(spread + 1.0) * (1.0 / math.sqrt(SEQ)))
-        row = lax.broadcasted_iota(jnp.int32, (group, width), 0) + at
-        col = lax.broadcasted_iota(jnp.int32, (group, width), 1)
-        normal = jnp.where((row >= first_row) & (col >= first_col), normal, 0.0)
-        for tile in range(tiles):
-            c_ref[tile, pl.ds(at, group), :] = normal[:, tile * LANES : (tile + 1) * LANES]
+        at = pl.multiple_of(number * group, 8)
+        contrast(at, 0, 0, 1, edge)
+        for tile in range(1, tiles, 2):
+            contrast(at, tile, LANES, 2, inside)
 
     out_ref[0] = jnp.full((q_count, m_count), -jnp.inf, jnp.float32)
 

time: 79.2 us -> 69.1 us (0.87)
  Pallas kernels: 76.9 us -> 66.7 us
    pallas_call x1, Pallas kernels: 30.6 us -> 20.4 us  [sequence_best(): pl.pallas_call(best_kernel, out_shape=jax.ShapeDtypeStruct((1, rows - LEA...]
where the time goes in v3:
time: 69.1 us; the launch traced here: 68.9 us
  Pallas kernels  66.7 us (97%)
  local copies, waits for them, and re-layouts  2.13 us (3%)
    pallas_call x1, Pallas kernels, score_tile(): pl.pallas_call(lambda *refs: score_kernel(npb, nma, chunks, *refs), out_s...  46.4 us
    pallas_call x1, Pallas kernels, sequence_best(): pl.pallas_call(best_kernel, out_shape=jax.ShapeDtypeStruct((1, rows - LEA...  20.4 us
    unnamed x6, local copies, waits for them, and re-layouts  2.13 us

profile of v3, /device:TPU:13, one launch (start us, length us, event | category | flops | bytes accessed | tf_op | source)
XLA Modules:
  0.0 68.9 jit_solution(17130968830070971352)
XLA Ops:
  0.0 0.0 copy-start
  0.0 1.2 %copy-done = bf16[1024,512]{1,0:T(8,128)(2,1)S(1)} copy-done((bf16[1024,512]{1,0:T(8,128)(2,1)S(1)}, bf16[1024,512]{1,0:T(8,128)(2,1)}, u32[]{:S(2)}) %copy-start) | copy-done | bytes 1048600
  1.2 0.0 copy-start.1
  1.2 0.9 %copy-done.1 = bf16[1,32,2048]{2,1,0:T(8,128)(2,1)S(1)} copy-done((bf16[1,32,2048]{2,1,0:T(8,128)(2,1)S(1)}, bf16[1,32,2048]{2,1,0:T(8,128)(2,1)}, u32[]{:S(2)}) %copy-start.1) | copy-done | bytes 131096
  2.1 0.0 copy-start.2
  2.1 46.4 %scores.1.ext_ref = f32[288,1536]{1,0:T(8,128)S(1)} custom-call(bf16[1,32,2048]{2,1,0:T(8,128)(2,1)S(1)} %copy-done.1, bf16[1024,512]{1,0:T(8,128)(2,1)S(1)} %copy-done), custom_call_target="tpu_custom_call" | custom-call | tf_op jit(solution)/shard_map/scores/pallas_call | solution.py:272
  48.5 0.0 copy-done.2
  48.5 20.4 %best.1 = f32[1,256,1024]{2,1,0:T(8,128)} custom-call(s32[8]{0:T(128)S(1)} %copy-done.2, f32[288,1536]{1,0:T(8,128)S(1)} %scores.1.ext_ref), custom_call_target="tpu_custom_call" | custom-call | tf_op jit(solution)/shard_map/best/pallas_call | solution.py:405
Async XLA Ops:
  0.0 1.2 %copy-start = (bf16[1024,512]{1,0:T(8,128)(2,1)S(1)}, bf16[1024,512]{1,0:T(8,128)(2,1)}, u32[]{:S(2)}) copy-start(bf16[1024,512]{1,0:T(8,128)(2,1)} %refs_1_.1) | copy-start | bytes 3145732
  1.2 0.9 %copy-start.1 = (bf16[1,32,2048]{2,1,0:T(8,128)(2,1)S(1)}, bf16[1,32,2048]{2,1,0:T(8,128)(2,1)}, u32[]{:S(2)}) copy-start(bf16[1,32,2048]{2,1,0:T(8,128)(2,1)} %refs_0_.1) | copy-start | bytes 393220
  2.1 46.4 %copy-start.2 = (s32[8]{0:T(128)S(1)}, s32[8]{0:T(128)}, u32[]{:S(2)}) copy-start(s32[8]{0:T(128)} %slopes_ref.1) | copy-start | bytes 100

commit v4 on v3

--- a/solution.py
+++ b/solution.py
@@ -125,7 +125,8 @@
             m_to_row[i, chunk] = remote(
                 piece(pb, chunk), piece(pb, chunk), m_send.at[at], m_recv.at[at], {"pb": other}
             )
-            m_to_row[i, chunk].start()
+            if chunk != order[-1]:
+                m_to_row[i, chunk].start()
     for chunk in order:
         at = (pair - 1) * chunks + chunk
         m_to_mate[-1, chunk] = remote(
@@ -153,6 +154,9 @@
     def _():
         lead.start()
 
+    for i in range(pair - 1):
+        m_to_row[i, order[-1]].start()
+
     @pl.when(pb == 0)
     def _():
         q_lead[...] = jnp.zeros_like(q_lead)
@@ -171,22 +175,56 @@
             return ref[...].reshape(count * each, width)
         return ref[...].astype(jnp.float32).reshape(count * each, width).astype(ref.dtype)
 
-    to_right = remote(
-        scores.at[:, pl.ds(m_count - LEFT, LEFT)],
-        left,
-        halo_send.at[0],
-        halo_recv.at[0],
-        {"ma": ma + 1},
-    )
-    to_left = remote(
-        scores.at[:, pl.ds(0, RIGHT)],
-        right,
-        halo_send.at[1],
-        halo_recv.at[1],
-        {"ma": ma - 1},
-    )
-    done = set()
+    q_count = nma * q_all.shape[1]
+    bands = ((LEAD, q_count), (0, LEAD))
+
+    def halo(number, begin, width, into, where):
+        rows = pl.ds(*bands[number % 2])
+        return remote(
+            scores.at[rows, pl.ds(begin, width)],
+            into.at[rows],
+            halo_send.at[number],
+            halo_recv.at[number],
+            {"ma": where},
+        )
+
+    to_right = [halo(i, m_count - LEFT, LEFT, left, ma + 1) for i in (0, 1)]
+    to_left = [halo(i, 0, RIGHT, right, ma - 1) for i in (2, 3)]
+    right_part = set(range(m_count - LEFT, m_count, LANES))
+    left_part = set(range(0, RIGHT, LANES))
+
+    def score(queries, at, chunk):
+        k = m_ref.shape[1]
+        block = flat(queries)
+        total = None
+        for slot in range(npb):
+            part = lax.dot_general(
+                block[:, slot * k : (slot + 1) * k],
+                m_all[slot, pl.ds(chunk * step, step), :],
+                (((1,), (1,)), ((), ())),
+                preferred_element_type=jnp.float32,
+            )
+            total = part if total is None else total + part
+        scores[pl.ds(at, block.shape[0]), pl.ds(chunk * step, step)] = total
+
+    def send(test, copy):
+        @pl.when(test)
+        def _():
+            copy.start()
+
+    done, sent = set(), set()
     for number, chunk in enumerate(order):
+        if number == chunks - 1:
+
+            @pl.when(has_up)
+            def _():
+                lead.wait_recv()
+
+            for known in order[:-1]:
+                score(q_lead, 0, known)
+            assert right_part <= done and left_part <= done
+            send(has_right, to_right[1])
+            send(has_left, to_left[1])
         for i, source in enumerate(rows_from):
             m_to_row[i, chunk].wait_recv()
             at = (pair + i) * chunks + chunk
@@ -196,52 +234,29 @@
             m_to_mate[i, chunk].start()
         for i in range(-1, pair - 1):
             m_to_mate[i, chunk].wait_recv()
-        if number == 0:
-
-            @pl.when(has_up)
-            def _():
-                lead.wait_recv()
-
-        k = m_ref.shape[1]
-        for queries, at in ((q_lead, 0), (q_all, LEAD)):
-            total = None
-            block = flat(queries)
-            for slot in range(npb):
-                part = lax.dot_general(
-                    block[:, slot * k : (slot + 1) * k],
-                    m_all[slot, pl.ds(chunk * step, step), :],
-                    (((1,), (1,)), ((), ())),
-                    preferred_element_type=jnp.float32,
-                )
-                total = part if total is None else total + part
-            scores[pl.ds(at, block.shape[0]), pl.ds(chunk * step, step)] = total
-        before = set(done)
+        score(q_all, LEAD, chunk)
         done.update(range(chunk * step, (chunk + 1) * step, LANES))
-        right_part = set(range(m_count - LEFT, m_count, LANES))
-        left_part = set(range(0, RIGHT, LANES))
-        if right_part <= done and not right_part <= before:
-
-            @pl.when(has_right)
-            def _():
-                to_right.start()
-
-        if left_part <= done and not left_part <= before:
-
-            @pl.when(has_left)
-            def _():
-                to_left.start()
+        if right_part <= done and "right" not in sent:
+            sent.add("right")
+            send(has_right, to_right[0])
+        if left_part <= done and "left" not in sent:
+            sent.add("left")
+            send(has_left, to_left[0])
+    score(q_lead, 0, order[-1])
 
     out_ref[:, pl.ds(LEFT, m_count)] = scores[...]
 
     @pl.when(has_left)
     def _():
-        to_right.wait_recv()
+        for copy in to_right:
+            copy.wait_recv()
 
     out_ref[:, pl.ds(0, LEFT)] = left[...]
 
     @pl.when(has_right)
     def _():
-        to_left.wait_recv()
+        for copy in to_left:
+            copy.wait_recv()
 
     out_ref[:, pl.ds(LEFT + m_count, RIGHT)] = right[...]
 
@@ -254,11 +269,13 @@
 
     @pl.when(has_right)
     def _():
-        to_right.wait_send()
+        for copy in to_right:
+            copy.wait_send()
 
     @pl.when(has_left)
     def _():
-        to_left.wait_send()
+        for copy in to_left:
+            copy.wait_send()
 
 
 def score_tile(queries, map_descriptors, npb, nma):
@@ -289,8 +306,8 @@
             dma((2,)),
             dma((2 * pair * chunks,)),
             dma((2 * pair * chunks,)),
-            dma((2,)),
-            dma((2,)),
+            dma((4,)),
+            dma((4,)),
         ],
         compiler_params=pltpu.CompilerParams(
             collective_id=0, has_side_effects=True, vmem_limit_bytes=48 << 20

time: 69.1 us -> 62.1 us (0.90)
  the two profiles are of different devices: /device:TPU:13 before, /device:TPU:0 now
where the time goes in v4:
time: 62.1 us; the launch traced here: 62 us
  Pallas kernels  59.8 us (96%)
  local copies, waits for them, and re-layouts  2.13 us (3%)
    pallas_call x1, Pallas kernels, score_tile(): pl.pallas_call(lambda *refs: score_kernel(npb, nma, chunks, *refs), out_s...  39.5 us
    pallas_call x1, Pallas kernels, sequence_best(): pl.pallas_call(best_kernel, out_shape=jax.ShapeDtypeStruct((1, rows - LEA...  20.4 us
    unnamed x6, local copies, waits for them, and re-layouts  2.13 us

profile of v4, /device:TPU:0, one launch (start us, length us, event | category | flops | bytes accessed | tf_op | source)
XLA Modules:
  0.0 62.0 jit_solution(5966257174501255988)
XLA Ops:
  0.0 0.0 copy-start
  0.0 1.2 %copy-done = bf16[1024,512]{1,0:T(8,128)(2,1)S(1)} copy-done((bf16[1024,512]{1,0:T(8,128)(2,1)S(1)}, bf16[1024,512]{1,0:T(8,128)(2,1)}, u32[]{:S(2)}) %copy-start) | copy-done | bytes 1048600
  1.2 0.0 copy-start.1
  1.2 0.9 %copy-done.1 = bf16[1,32,2048]{2,1,0:T(8,128)(2,1)S(1)} copy-done((bf16[1,32,2048]{2,1,0:T(8,128)(2,1)S(1)}, bf16[1,32,2048]{2,1,0:T(8,128)(2,1)}, u32[]{:S(2)}) %copy-start.1) | copy-done | bytes 131096
  2.1 0.0 copy-start.2
  2.1 39.5 %scores.1.ext_ref = f32[288,1536]{1,0:T(8,128)S(1)} custom-call(bf16[1,32,2048]{2,1,0:T(8,128)(2,1)S(1)} %copy-done.1, bf16[1024,512]{1,0:T(8,128)(2,1)S(1)} %copy-done), custom_call_target="tpu_custom_call" | custom-call | tf_op jit(solution)/shard_map/scores/pallas_call | solution.py:289
  41.6 0.0 copy-done.2
  41.6 20.4 %best.1 = f32[1,256,1024]{2,1,0:T(8,128)} custom-call(s32[8]{0:T(128)S(1)} %copy-done.2, f32[288,1536]{1,0:T(8,128)S(1)} %scores.1.ext_ref), custom_call_target="tpu_custom_call" | custom-call | tf_op jit(solution)/shard_map/best/pallas_call | solution.py:422
Async XLA Ops:
  0.0 1.2 %copy-start = (bf16[1024,512]{1,0:T(8,128)(2,1)S(1)}, bf16[1024,512]{1,0:T(8,128)(2,1)}, u32[]{:S(2)}) copy-start(bf16[1024,512]{1,0:T(8,128)(2,1)} %refs_1_.1) | copy-start | bytes 3145732
  1.2 0.9 %copy-start.1 = (bf16[1,32,2048]{2,1,0:T(8,128)(2,1)S(1)}, bf16[1,32,2048]{2,1,0:T(8,128)(2,1)}, u32[]{:S(2)}) copy-start(bf16[1,32,2048]{2,1,0:T(8,128)(2,1)} %refs_0_.1) | copy-start | bytes 393220
  2.1 39.5 %copy-start.2 = (s32[8]{0:T(128)S(1)}, s32[8]{0:T(128)}, u32[]{:S(2)}) copy-start(s32[8]{0:T(128)} %slopes_ref.1) | copy-start | bytes 100

commit v5 on v4

--- a/solution.py
+++ b/solution.py
@@ -206,6 +206,7 @@
             )
             total = part if total is None else total + part
         scores[pl.ds(at, block.shape[0]), pl.ds(chunk * step, step)] = total
+        out_ref[pl.ds(at, block.shape[0]), pl.ds(LEFT + chunk * step, step)] = total
 
     def send(test, copy):
         @pl.when(test)
@@ -244,7 +245,6 @@
             send(has_left, to_left[0])
     score(q_lead, 0, order[-1])
 
-    out_ref[:, pl.ds(LEFT, m_count)] = scores[...]
 
     @pl.when(has_left)
     def _():
@@ -282,7 +282,7 @@
     each, width = queries.shape[1:]
     m_count, k = map_descriptors.shape
     q_count = each * nma
-    chunks = 4
+    chunks = 8
     held = LEAD // each
     pair, across = npb // CORES, nma // 2
     dma = pltpu.SemaphoreType.DMA

time: 62.1 us -> 64.1 us (1.032)
  the two profiles are of different devices: /device:TPU:0 before, /device:TPU:13 now
where the time goes in v5:
time: 64.1 us; the launch traced here: 62.9 us
  Pallas kernels  60.7 us (95%)
  local copies, waits for them, and re-layouts  2.13 us (3%)
    pallas_call x1, Pallas kernels, score_tile(): pl.pallas_call(lambda *refs: score_kernel(npb, nma, chunks, *refs), out_s...  40.3 us
    pallas_call x1, Pallas kernels, sequence_best(): pl.pallas_call(best_kernel, out_shape=jax.ShapeDtypeStruct((1, rows - LEA...  20.4 us
    unnamed x6, local copies, waits for them, and re-layouts  2.13 us

profile of v5, /device:TPU:13, one launch (start us, length us, event | category | flops | bytes accessed | tf_op | source)
XLA Modules:
  0.0 62.9 jit_solution(11239241517409009575)
XLA Ops:
  0.0 0.0 copy-start
  0.0 1.2 %copy-done = bf16[1024,512]{1,0:T(8,128)(2,1)S(1)} copy-done((bf16[1024,512]{1,0:T(8,128)(2,1)S(1)}, bf16[1024,512]{1,0:T(8,128)(2,1)}, u32[]{:S(2)}) %copy-start) | copy-done | bytes 1048600
  1.2 0.0 copy-start.1
  1.2 0.9 %copy-done.1 = bf16[1,32,2048]{2,1,0:T(8,128)(2,1)S(1)} copy-done((bf16[1,32,2048]{2,1,0:T(8,128)(2,1)S(1)}, bf16[1,32,2048]{2,1,0:T(8,128)(2,1)}, u32[]{:S(2)}) %copy-start.1) | copy-done | bytes 131096
  2.1 0.0 copy-start.2
  2.1 40.3 %scores.1.ext_ref = f32[288,1536]{1,0:T(8,128)S(1)} custom-call(bf16[1,32,2048]{2,1,0:T(8,128)(2,1)S(1)} %copy-done.1, bf16[1024,512]{1,0:T(8,128)(2,1)S(1)} %copy-done), custom_call_target="tpu_custom_call" | custom-call | tf_op jit(solution)/shard_map/scores/pallas_call | solution.py:289
  42.5 0.0 copy-done.2
  42.5 20.4 %best.1 = f32[1,256,1024]{2,1,0:T(8,128)} custom-call(s32[8]{0:T(128)S(1)} %copy-done.2, f32[288,1536]{1,0:T(8,128)S(1)} %scores.1.ext_ref), custom_call_target="tpu_custom_call" | custom-call | tf_op jit(solution)/shard_map/best/pallas_call | solution.py:422
Async XLA Ops:
  0.0 1.2 %copy-start = (bf16[1024,512]{1,0:T(8,128)(2,1)S(1)}, bf16[1024,512]{1,0:T(8,128)(2,1)}, u32[]{:S(2)}) copy-start(bf16[1024,512]{1,0:T(8,128)(2,1)} %refs_1_.1) | copy-start | bytes 3145732
  1.2 0.9 %copy-start.1 = (bf16[1,32,2048]{2,1,0:T(8,128)(2,1)S(1)}, bf16[1,32,2048]{2,1,0:T(8,128)(2,1)}, u32[]{:S(2)}) copy-start(bf16[1,32,2048]{2,1,0:T(8,128)(2,1)} %refs_0_.1) | copy-start | bytes 393220
  2.1 40.3 %copy-start.2 = (s32[8]{0:T(128)S(1)}, s32[8]{0:T(128)}, u32[]{:S(2)}) copy-start(s32[8]{0:T(128)} %slopes_ref.1) | copy-start | bytes 100

commit v6 on v5

--- a/solution.py
+++ b/solution.py
@@ -282,7 +282,7 @@
     each, width = queries.shape[1:]
     m_count, k = map_descriptors.shape
     q_count = each * nma
-    chunks = 8
+    chunks = 4
     held = LEAD // each
     pair, across = npb // CORES, nma // 2
     dma = pltpu.SemaphoreType.DMA

time: 64.1 us -> 62.1 us (0.969)
  the two profiles are of different devices: /device:TPU:13 before, /device:TPU:0 now
where the time goes in v6:
time: 62.1 us; the launch traced here: 62 us
  Pallas kernels  59.8 us (96%)
  local copies, waits for them, and re-layouts  2.13 us (3%)
    pallas_call x1, Pallas kernels, score_tile(): pl.pallas_call(lambda *refs: score_kernel(npb, nma, chunks, *refs), out_s...  39.5 us
    pallas_call x1, Pallas kernels, sequence_best(): pl.pallas_call(best_kernel, out_shape=jax.ShapeDtypeStruct((1, rows - LEA...  20.4 us
    unnamed x6, local copies, waits for them, and re-layouts  2.13 us

profile of v6, /device:TPU:0, one launch (start us, length us, event | category | flops | bytes accessed | tf_op | source)
XLA Modules:
  0.0 62.0 jit_solution(5615485144907444779)
XLA Ops:
  0.0 0.0 copy-start
  0.0 1.2 %copy-done = bf16[1024,512]{1,0:T(8,128)(2,1)S(1)} copy-done((bf16[1024,512]{1,0:T(8,128)(2,1)S(1)}, bf16[1024,512]{1,0:T(8,128)(2,1)}, u32[]{:S(2)}) %copy-start) | copy-done | bytes 1048600
  1.2 0.0 copy-start.1
  1.2 0.9 %copy-done.1 = bf16[1,32,2048]{2,1,0:T(8,128)(2,1)S(1)} copy-done((bf16[1,32,2048]{2,1,0:T(8,128)(2,1)S(1)}, bf16[1,32,2048]{2,1,0:T(8,128)(2,1)}, u32[]{:S(2)}) %copy-start.1) | copy-done | bytes 131096
  2.1 0.0 copy-start.2
  2.1 39.5 %scores.1.ext_ref = f32[288,1536]{1,0:T(8,128)S(1)} custom-call(bf16[1,32,2048]{2,1,0:T(8,128)(2,1)S(1)} %copy-done.1, bf16[1024,512]{1,0:T(8,128)(2,1)S(1)} %copy-done), custom_call_target="tpu_custom_call" | custom-call | tf_op jit(solution)/shard_map/scores/pallas_call | solution.py:289
  41.6 0.0 copy-done.2
  41.6 20.4 %best.1 = f32[1,256,1024]{2,1,0:T(8,128)} custom-call(s32[8]{0:T(128)S(1)} %copy-done.2, f32[288,1536]{1,0:T(8,128)S(1)} %scores.1.ext_ref), custom_call_target="tpu_custom_call" | custom-call | tf_op jit(solution)/shard_map/best/pallas_call | solution.py:422
Async XLA Ops:
  0.0 1.2 %copy-start = (bf16[1024,512]{1,0:T(8,128)(2,1)S(1)}, bf16[1024,512]{1,0:T(8,128)(2,1)}, u32[]{:S(2)}) copy-start(bf16[1024,512]{1,0:T(8,128)(2,1)} %refs_1_.1) | copy-start | bytes 3145732
  1.2 0.9 %copy-start.1 = (bf16[1,32,2048]{2,1,0:T(8,128)(2,1)S(1)}, bf16[1,32,2048]{2,1,0:T(8,128)(2,1)}, u32[]{:S(2)}) copy-start(bf16[1,32,2048]{2,1,0:T(8,128)(2,1)} %refs_0_.1) | copy-start | bytes 393220
  2.1 39.5 %copy-start.2 = (s32[8]{0:T(128)S(1)}, s32[8]{0:T(128)}, u32[]{:S(2)}) copy-start(s32[8]{0:T(128)} %slopes_ref.1) | copy-start | bytes 100
